TPU v7x, 256 devices: a whole 4x4x8 slice. The times are simulated.
256 devices in a mesh: front: 64 (over z, y, core), sect: 4 (over x).
Axes of the slice: x: 4, y: 4, z: 8, core: 2. Of those that a mesh axis runs over, the one named last changes fastest.
Arguments:
- pivot_rows: float32 [64, 4, 512, 512], P('front', 'sect'), may hold values from -6 to 6
- sections: float32 [64, 4, 4, 256, 512], P('front', 'sect'), may hold values from -6 to 6
- sect_vectors: bfloat16 [64, 4, 4, 256, 512], P('front', 'sect'), may hold values from -0.375 to 0.375
- sect_factors: bfloat16 [64, 4, 4, 512, 512], P('front', 'sect'), may hold values from -0.125 to 0.125
- routes: int32 [64, 4, 1024, 1], P('front', 'sect'), may hold values from 0 to 63; in each aligned block of 1024 rows (0 to 1023, 1024 to 2047, ..., all dimensions but the last counted through in order) at most 24 rows name the same one
- parent_vectors: bfloat16 [64, 4, 1536, 512], P('front', 'sect'), may hold values from -0.078125 to 0.078125
- parent_factor: bfloat16 [64, 512, 512], P('front'), may hold values from -0.25 to 0.25
Outputs:
- top_rows: float32 [64, 4, 512, 512], P('front', 'sect')
- parent_rows: float32 [64, 4, 1536, 512], P('front', 'sect')
Inputs may be any that keep to these rules, and one draw needn't show every extreme that they name: `routes`: the rows of one section name each parent owner at most 24 times, a bound that some block reaches.
All inputs are finite; a program needn't handle non-finite values.
Results may differ from a plain program's by a relative error of at most 0.0003.
Values sent between devices are 32-bit elements; how exact they have to be, the bound alone decides.
No kernel may reach another device: no remote copies, remote signals or barrier semaphores. Data moves between devices by JAX's collectives and lax.ppermute only.
A program may use at most 128 MiB of HBM per device.

v0:
```python
import functools

import jax
import jax.numpy as jnp
from jax import lax
from jax.experimental import pallas as pl
from jax.experimental.pallas import tpu as pltpu
from jax.sharding import PartitionSpec as P


CHUNKS = (((0, 128), (128, 128)), ((256, 128), (384, 128)))
MIB = 1 << 20


def passed_along(value, steps):
    count = lax.axis_size("sect")
    pairs = [(source, (source + steps) % count) for source in range(count)]
    return lax.ppermute(value, "sect", pairs)


def halves(value):
    high = value.astype(jnp.bfloat16)
    low = (value - high.astype(jnp.float32)).astype(jnp.bfloat16)
    return high, low


def product(left, right, axis):
    width = right.shape[1]
    dot = functools.partial(
        lax.dot_general,
        dimension_numbers=(((axis,), (0,)), ((), ())),
        preferred_element_type=jnp.float32,
    )
    high, low = halves(right)
    if width < 256:
        both = dot(left, jnp.concatenate([low, high], axis=1))
        return both[:, :width] + both[:, width:]
    return dot(left, low) + dot(left, high)


def first_kernel(panel, pivot, block, vectors, factor, pivot_out, block_out):
    change = product(factor[0], pivot[...] + product(vectors[0], block[0], 0), 0)
    pivot_out[...] = pivot[...] - change
    block_out[...] = block[0] - product(vectors[0], change, 1)


def reflect_kernel(step, panel, pivot, block, vectors, turned, factor, pivot_out, block_out):
    change = product(factor[step], pivot[...] + product(turned[step], block[0], 1), 1)
    pivot_out[...] = pivot[...] - change
    block_out[...] = block[0] - product(vectors[step], change, 1)


def place_rows(slots, base, blocks, out):
    @pl.loop(0, blocks[0].shape[0] // 16)
    def _(group):
        for inner in range(16):
            row = group * 16 + inner
            pieces = [block[pl.ds(row, 1), :] for block in blocks]
            value = jnp.concatenate(pieces, axis=1) if len(pieces) > 1 else pieces[0]
            out[pl.ds(slots[base + row], 1), :] = value


def last_kernel(step, panel, slots, pivot, block, vectors, turned, factor, packed, *refs):
    *others, pivot_out, packed_out, updated = refs
    packed_out[...] = packed[...]
    reflect_kernel(step, panel, pivot, block, vectors, turned, factor, pivot_out, updated)
    place_rows(slots, panel[0] * updated.shape[0], [*others, updated], packed_out)


def reflect(panel, step, pivot, column, width, sections, weights):
    rows = sections.shape[1]
    size = pivot.shape[0]
    at = column // width
    if len(weights) == 2:
        body = first_kernel
        weight_specs = [
            pl.BlockSpec((1, rows, size), lambda i, p: (p[0], 0, 0)),
            pl.BlockSpec((1, size, size), lambda i, p: (p[0], 0, 0)),
        ]
    else:
        body = functools.partial(reflect_kernel, step)
        weight_specs = [pl.BlockSpec(memory_space=pltpu.VMEM)] * 3
    pivot_at = at if step == 0 else 0
    return pl.pallas_call(
        body,
        grid_spec=pltpu.PrefetchScalarGridSpec(
            num_scalar_prefetch=1,
            grid=(1,),
            in_specs=[
                pl.BlockSpec((size, width), lambda i, p: (0, pivot_at)),
                pl.BlockSpec((1, rows, width), lambda i, p: (p[0], 0, at)),
                *weight_specs,
            ],
            out_specs=[
                pl.BlockSpec((size, width), lambda i, p: (0, 0)),
                pl.BlockSpec((rows, width), lambda i, p: (0, 0)),
            ],
        ),
        out_shape=[
            jax.ShapeDtypeStruct((size, width), jnp.float32),
            jax.ShapeDtypeStruct((rows, width), jnp.float32),
        ],
        cost_estimate=pl.CostEstimate(
            flops=4 * width * size * (2 * rows + size),
            bytes_accessed=4 * width * 2 * (size + rows) + 2 * size * (rows + size),
            transcendentals=0,
        ),
        compiler_params=pltpu.CompilerParams(vmem_limit_bytes=16 * MIB),
        name="reflect",
    )(panel, pivot, sections, *weights)


def reflect_last(panel, step, slots, pivot, column, sections, weights, packed, others):
    rows = sections.shape[1]
    size, width = pivot.shape
    total, wide = packed.shape
    at = column // width
    return pl.pallas_call(
        functools.partial(last_kernel, step),
        grid_spec=pltpu.PrefetchScalarGridSpec(
            num_scalar_prefetch=2,
            grid=(1,),
            in_specs=[
                pl.BlockSpec((size, width), lambda i, p, s: (0, 0)),
                pl.BlockSpec((1, rows, width), lambda i, p, s: (p[0], 0, at)),
                *[pl.BlockSpec(memory_space=pltpu.VMEM)] * 3,
                pl.BlockSpec((total, wide), lambda i, p, s: (0, 0)),
                *[pl.BlockSpec(other.shape, lambda i, p, s: (0, 0)) for other in others],
            ],
            out_specs=[
                pl.BlockSpec((size, width), lambda i, p, s: (0, 0)),
                pl.BlockSpec((total, wide), lambda i, p, s: (0, 0)),
            ],
            scratch_shapes=[pltpu.VMEM((rows, width), jnp.float32)],
        ),
        out_shape=[
            pltpu.HBM((size, width), jnp.float32),
            pltpu.HBM((total, wide), jnp.float32),
        ],
        cost_estimate=pl.CostEstimate(
            flops=4 * width * size * (2 * rows + size),
            bytes_accessed=8 * width * (size + rows) + 8 * wide * total + 2 * size * (rows + size),
            transcendentals=0,
        ),
        compiler_params=pltpu.CompilerParams(vmem_limit_bytes=16 * MIB),
        name="reflect_last",
    )(panel, slots, pivot, sections, *weights, packed, *others)


def stage_kernel(panels, vectors, factor, vectors_out, turned_out, factor_out):
    step = pl.program_id(0)
    vectors_out[step] = vectors[0]
    turned_out[step] = vectors[0].T
    factor_out[step] = factor[0].T


def stage(panels, vectors, factors):
    count, rows, size = vectors.shape
    whole = pl.BlockSpec(memory_space=pltpu.VMEM)
    return pl.pallas_call(
        stage_kernel,
        grid_spec=pltpu.PrefetchScalarGridSpec(
            num_scalar_prefetch=1,
            grid=(count,),
            in_specs=[
                pl.BlockSpec((1, rows, size), lambda i, p: (p[i], 0, 0)),
                pl.BlockSpec((1, size, size), lambda i, p: (p[i], 0, 0)),
            ],
            out_specs=[whole, whole, whole],
        ),
        out_shape=[
            pltpu.VMEM((count, rows, size), vectors.dtype),
            pltpu.VMEM((count, size, rows), vectors.dtype),
            pltpu.VMEM((count, size, size), vectors.dtype),
        ],
        cost_estimate=pl.CostEstimate(
            flops=0, bytes_accessed=2 * count * size * (rows + size), transcendentals=0
        ),
        compiler_params=pltpu.CompilerParams(vmem_limit_bytes=16 * MIB),
        name="stage",
    )(panels, vectors, factors)


def pack_kernel(steps, bases, slots, *refs):
    blocks, out = refs[:-1], refs[-1]
    out[...] = jnp.zeros_like(out)
    for step in range(steps):
        place_rows(slots, bases[step], blocks[step::steps], out)


def pack(bases, slots, streams, total):
    blocks = [block for stream in streams for block in stream]
    wide = sum(stream[0].shape[1] for stream in streams)
    return pl.pallas_call(
        functools.partial(pack_kernel, len(streams[0])),
        grid_spec=pltpu.PrefetchScalarGridSpec(
            num_scalar_prefetch=2,
            grid=(1,),
            in_specs=[pl.BlockSpec(b.shape, lambda i, *_: (0, 0)) for b in blocks],
            out_specs=pl.BlockSpec((total, wide), lambda i, *_: (0, 0)),
        ),
        out_shape=jax.ShapeDtypeStruct((total, wide), jnp.float32),
        cost_estimate=pl.CostEstimate(
            flops=total * wide, bytes_accessed=6 * wide * total, transcendentals=0
        ),
        compiler_params=pltpu.CompilerParams(vmem_limit_bytes=16 * MIB),
        name="pack",
    )(bases, slots, *blocks)


def project_kernel(owner, vectors, rows, *outs):
    scratch = outs[-1]
    scratch[...] = product(vectors[...], rows[...], 0)
    count = len(outs) - 1
    part = scratch.shape[0] // count
    for away in range(count):
        start = pl.multiple_of(lax.rem(owner[0] + away, count) * part, part)
        outs[away][...] = scratch[pl.ds(start, part), :]


def project(owner, vectors, rows, count):
    total, width = rows.shape
    size = vectors.shape[1]
    part = size // count
    return pl.pallas_call(
        project_kernel,
        grid_spec=pltpu.PrefetchScalarGridSpec(
            num_scalar_prefetch=1,
            grid=(1,),
            in_specs=[
                pl.BlockSpec((total, size), lambda i, p: (0, 0)),
                pl.BlockSpec((total, width), lambda i, p: (0, 0)),
            ],
            out_specs=[pl.BlockSpec((part, width), lambda i, p: (0, 0))] * count,
            scratch_shapes=[pltpu.VMEM((size, width), jnp.float32)],
        ),
        out_shape=[jax.ShapeDtypeStruct((part, width), jnp.float32)] * count,
        cost_estimate=pl.CostEstimate(
            flops=4 * total * size * width,
            bytes_accessed=4 * width * (total + size) + 2 * total * size,
            transcendentals=0,
        ),
        compiler_params=pltpu.CompilerParams(vmem_limit_bytes=16 * MIB),
        name="project",
    )(owner, vectors, rows)


def finish_kernel(refs_parts, owner, factor, vectors, rows, *refs):
    out, scratch = refs[-2:]
    count = refs_parts
    parts = refs[:count]
    part = scratch.shape[0] // count

    @pl.when(pl.program_id(0) == 0)
    def _():
        for away in range(count):
            start = pl.multiple_of(lax.rem(owner[0] + count - away, count) * part, part)
            scratch[pl.ds(start, part), :] = parts[away][...]
        scratch[...] = product(factor[...], scratch[...], 0)

    out[...] = rows[...] - product(vectors[...], scratch[...], 1)


def finish(owner, factor, vectors, rows, parts, whole, column, columns):
    total, width = rows.shape
    size = vectors.shape[1]
    tile = total // 4
    kept = [] if whole is None else [whole]
    return pl.pallas_call(
        functools.partial(finish_kernel, len(parts)),
        grid_spec=pltpu.PrefetchScalarGridSpec(
            num_scalar_prefetch=1,
            grid=(total // tile,),
            in_specs=[
                pl.BlockSpec((size, size), lambda i, p: (0, 0)),
                pl.BlockSpec((tile, size), lambda i, p: (i, 0)),
                pl.BlockSpec((tile, width), lambda i, p: (i, 0)),
                *[pl.BlockSpec(q.shape, lambda i, p: (0, 0)) for q in parts],
                *[pl.BlockSpec(memory_space=pl.ANY) for _ in kept],
            ],
            out_specs=pl.BlockSpec((tile, width), lambda i, p: (i, column)),
            scratch_shapes=[pltpu.VMEM((size, width), jnp.float32)],
        ),
        out_shape=jax.ShapeDtypeStruct((total, columns), jnp.float32),
        input_output_aliases={4 + len(parts): 0} if kept else {},
        cost_estimate=pl.CostEstimate(
            flops=4 * size * width * (total + size),
            bytes_accessed=4 * width * (2 * total + size) + 2 * size * (total + size),
            transcendentals=0,
        ),
        compiler_params=pltpu.CompilerParams(vmem_limit_bytes=16 * MIB),
        name="finish",
    )(owner, factor, vectors, rows, *parts, *kept)


def join_kernel(columns, *refs):
    for column, ref in zip(columns, refs[:-1]):
        refs[-1][:, column : column + ref.shape[1]] = ref[...]


def join(columns, pieces):
    size, total = pieces[0].shape[0], sum(piece.shape[1] for piece in pieces)
    tile = size // 2
    return pl.pallas_call(
        functools.partial(join_kernel, columns),
        grid=(2,),
        in_specs=[pl.BlockSpec((tile, piece.shape[1]), lambda i: (i, 0)) for piece in pieces],
        out_specs=pl.BlockSpec((tile, total), lambda i: (i, 0)),
        out_shape=jax.ShapeDtypeStruct((size, total), jnp.float32),
        cost_estimate=pl.CostEstimate(flops=0, bytes_accessed=8 * size * total, transcendentals=0),
        compiler_params=pltpu.CompilerParams(vmem_limit_bytes=16 * MIB),
        name="join",
    )(*pieces)


def slots_of(destination, owners, capacity):
    onehot = destination[:, None] == jnp.arange(owners, dtype=jnp.int32)[None, :]
    onehot = onehot.astype(jnp.float32).reshape(-1, 128, owners)
    lower = jnp.tril(jnp.ones((128, 128), jnp.float32), -1)
    within = jnp.einsum("rs,bso->bro", lower, onehot)
    sums = jnp.sum(onehot, axis=1)
    ahead = jnp.cumsum(sums, axis=0) - sums
    rank = jnp.sum((within + ahead[:, None, :]) * onehot, axis=2)
    return destination * capacity + rank.reshape(-1).astype(jnp.int32)


def local(pivot_rows, sections, sect_vectors, sect_factors, routes, parent_vectors, parent_factor):
    me = lax.axis_index("sect")
    count = lax.axis_size("sect")
    owners = lax.axis_size("front")
    pivots = in_hbm(pivot_rows[0, 0])
    sections, sect_vectors = in_hbm(sections[0, 0]), in_hbm(sect_vectors[0, 0])
    sect_factors = in_hbm(sect_factors[0, 0])
    panels, rows = sections.shape[:2]
    capacity = 3 * panels * rows // (2 * owners)
    total = owners * capacity
    panel_at = [((me - step) % count).astype(jnp.int32)[None] for step in range(count)]
    slots = slots_of(routes[0, 0, :, 0], owners, capacity)
    bases = jnp.concatenate(panel_at) * rows
    owner = me.astype(jnp.int32)[None]
    vectors, factor = parent_vectors[0, 0], parent_factor[0]
    weights = stage(jnp.concatenate(panel_at), sect_vectors, sect_factors)
    tops, out = [], None
    for chunk, streams in enumerate(CHUNKS):
        column, width = streams[0][0], sum(width for _, width in streams)
        updated, moving = [], []
        for first, narrow in streams:
            pivot, blocks = pivots, []
            for step in range(count - 1):
                direct = chunk == 0 and step == 0
                pivot, block = reflect(
                    panel_at[step], step, pivot, first, narrow, sections,
                    (sect_vectors, sect_factors) if direct else weights,
                )
                blocks.append(block)
                pivot = passed_along(pivot, 1)
            updated.append(blocks)
            moving.append(pivot)
        packed = pack(bases, slots, updated, total)
        others = []
        for stream, (first, narrow) in enumerate(streams):
            last = stream == len(streams) - 1
            if last:
                pivot, packed = reflect_last(
                    panel_at[-1], count - 1, slots, moving[stream], first, sections, weights,
                    packed, others,
                )
            else:
                pivot, block = reflect(
                    panel_at[-1], count - 1, moving[stream], first, narrow, sections, weights
                )
                others.append(block)
            tops.append(passed_along(pivot, 1))
        arrived = lax.all_to_all(
            packed.reshape(owners, capacity, width), "front", split_axis=0, concat_axis=0, tiled=True
        ).reshape(total, width)
        own, *others = project(owner, vectors, arrived, count)
        others = [passed_along(part, away + 1) for away, part in enumerate(others)]
        for part in others:
            own = own + part
        parts = [own] + [passed_along(own, away) for away in range(1, count)]
        out = finish(owner, factor, vectors, arrived, parts, out, column // width, sections.shape[-1])
    top = join([column for streams in CHUNKS for column, _ in streams], tops)
    return (top[None, None], out[None, None])


def in_hbm(value):
    return pltpu.with_memory_space_constraint(value, pltpu.HBM)


def solution(mesh):
    in_specs = (
        P("front", "sect", None, None),
        P("front", "sect", None, None, None),
        P("front", "sect", None, None, None),
        P("front", "sect", None, None, None),
        P("front", "sect", None, None),
        P("front", "sect", None, None),
        P("front", None, None),
    )
    out_specs = (P("front", "sect", None, None), P("front", "sect", None, None))
    return jax.shard_map(local, mesh=mesh, in_specs=in_specs, out_specs=out_specs, check_vma=False)
```

profile of v0, /device:TPU:8, one launch (start us, length us, event | category | flops | bytes accessed | tf_op | source)
XLA Modules:
  0.0 193.3 jit_solution(5440712991273315254)
XLA Ops:
  0.6 2.6 %reflect.14 = (f32[512,128]{1,0:T(8,128)}, f32[256,128]{1,0:T(8,128)S(1)}) custom-call(s32[1]{0:T(128)} %bitcast.3.panel, f32[512,512]{1,0:T(8,128)} %bitcast.57, f32[4,256,512]{2,1,0:T(8,128)} %bitcast.38, bf16[4,256,512]{2,1,0:T(8,128)(2,1)} %bitcast.62, bf16[4,512,512]{2,1,0:T(8,128)(2,1)} %bitcast.54), custom_call_target="tpu_custom_call" | custom-call | flops 268435456 | bytes 1572864 | tf_op jit(solution)/shard_map/reflect/pallas_call | solution.py:84
  4.8 2.6 %reflect.18 = (f32[512,128]{1,0:T(8,128)}, f32[256,128]{1,0:T(8,128)S(1)}) custom-call(s32[1]{0:T(128)} %bitcast.3.panel, f32[512,512]{1,0:T(8,128)} %bitcast.58, f32[4,256,512]{2,1,0:T(8,128)} %bitcast.39, bf16[4,256,512]{2,1,0:T(8,128)(2,1)} %bitcast.63, bf16[4,512,512]{2,1,0:T(8,128)(2,1)} %bitcast.55), custom_call_target="tpu_custom_call" | custom-call | flops 268435456 | bytes 1572864 | tf_op jit(solution)/shard_map/reflect/pallas_call | solution.py:84
  9.6 3.7 %stage.1 = (bf16[4,256,512]{2,1,0:T(8,128)(2,1)S(1)}, bf16[4,512,256]{2,1,0:T(8,128)(2,1)S(1)}, bf16[4,512,512]{2,1,0:T(8,128)(2,1)S(1)}) custom-call(s32[4]{0:T(128)S(1)} %get-tuple-element.89.panels, bf16[4,256,512]{2,1,0:T(8,128)(2,1)} %bitcast.64, bf16[4,512,512]{2,1,0:T(8,128)(2,1)} %bitcast.56), custom_call_target="tpu_custom_call" | custom-call | bytes 3145728 | tf_op jit(solution)/shard_map/stage/pallas_call | solution.py:160
  22.1 3.6 %collective-permute-done.1.pivot = f32[512,128]{1,0:T(8,128)} collective-permute-done((f32[512,128]{1,0:T(8,128)}, f32[512,128]{1,0:T(8,128)}, u32[]{:S(2)}, u32[]{:S(2)}) %collective-permute-start.1) | collective-permute-done | bytes 262176 | tf_op jit(solution)/shard_map/ppermute | solution.py:18
  34.0 2.6 %pack.2.packed = f32[1536,256]{1,0:T(8,128)S(1)} custom-call(s32[4]{0:T(128)S(1)} %get-tuple-element.88.bases, s32[1024]{0:T(1024)S(1)} %bitcast_add_fusion.slots, f32[256,128]{1,0:T(8,128)S(1)} %get-tuple-element.55.refs_0_, f32[256,128]{1,0:T(8,128)S(1)} %copy-done.10, f32[256,128]{1,0:T(8,128)S(1)} %get-tuple-element.57.refs_2_, ...), custom_call_target="tpu_custom_call" | custom-call | flops 393216 | bytes 2359296 | tf_op jit(solution)/shard_map/pack/pallas_call | solution.py:194
  39.6 2.4 %collective-permute-done.6.pivot = f32[512,128]{1,0:T(8,128)S(1)} collective-permute-done((f32[512,128]{1,0:T(8,128)S(1)}, f32[512,128]{1,0:T(8,128)S(1)}, u32[]{:S(2)}, u32[]{:S(2)}) %collective-permute-start.6) | collective-permute-done | bytes 262176 | tf_op jit(solution)/shard_map/ppermute | solution.py:18
  42.0 4.3 %reflect_last.2 = (f32[512,128]{1,0:T(8,128)}, f32[1536,256]{1,0:T(8,128)}) custom-call(s32[1]{0:T(128)} %bitcast.panel, s32[1024]{0:T(1024)S(1)} %bitcast_add_fusion.slots, f32[512,128]{1,0:T(8,128)S(1)} %collective-permute-done.6.pivot, f32[4,256,512]{2,1,0:T(8,128)} %bitcast.45, bf16[4,256,512]{2,1,0:T(8,128)(2,1)S(1)} %get-tuple-element.46.vectors, ...), custom_call_target="tpu_custom_call" | custom-call | flops 268435456 | bytes 4718592 | tf_op jit(solution)/shard_map/reflect_last/pallas_call | solution.py:118
  46.3 12.3 %all-to-all-start.1 = ((f32[64,24,256]{2,1,0:T(8,128)}), f32[64,24,256]{2,1,0:T(8,128)}, u32[]{:S(2)}, u32[]{:S(2)}) async-start(f32[64,24,256]{2,1,0:T(8,128)} %bitcast.65), calls=%async_computation.1 | async-start | bytes 3145728 | tf_op jit(solution)/shard_map/all_to_all | solution.py:374
  64.3 7.9 %collective-permute-done.8.pivot = f32[512,128]{1,0:T(8,128)S(1)} collective-permute-done((f32[512,128]{1,0:T(8,128)S(1)}, f32[512,128]{1,0:T(8,128)S(1)}, u32[]{:S(2)}, u32[]{:S(2)}) %collective-permute-start.8) | collective-permute-done | bytes 262176 | tf_op jit(solution)/shard_map/ppermute | solution.py:18
  74.0 3.6 %collective-permute-done.12.pivot = f32[512,128]{1,0:T(8,128)S(1)} collective-permute-done((f32[512,128]{1,0:T(8,128)S(1)}, f32[512,128]{1,0:T(8,128)S(1)}, u32[]{:S(2)}, u32[]{:S(2)}) %collective-permute-start.12) | collective-permute-done | bytes 262176 | tf_op jit(solution)/shard_map/ppermute | solution.py:18
  79.4 3.8 %collective-permute-done.9.pivot = f32[512,128]{1,0:T(8,128)S(1)} collective-permute-done((f32[512,128]{1,0:T(8,128)S(1)}, f32[512,128]{1,0:T(8,128)S(1)}, u32[]{:S(2)}, u32[]{:S(2)}) %collective-permute-start.9) | collective-permute-done | bytes 262176 | tf_op jit(solution)/shard_map/ppermute | solution.py:18
  85.1 4.8 %collective-permute-done.13.pivot = f32[512,128]{1,0:T(8,128)S(1)} collective-permute-done((f32[512,128]{1,0:T(8,128)S(1)}, f32[512,128]{1,0:T(8,128)S(1)}, u32[]{:S(2)}, u32[]{:S(2)}) %collective-permute-start.13) | collective-permute-done | bytes 262176 | tf_op jit(solution)/shard_map/ppermute | solution.py:18
  91.6 2.6 %pack.3.packed = f32[1536,256]{1,0:T(8,128)S(1)} custom-call(s32[4]{0:T(128)S(1)} %get-tuple-element.88.bases, s32[1024]{0:T(1024)S(1)} %bitcast_add_fusion.slots, f32[256,128]{1,0:T(8,128)S(1)} %get-tuple-element.70.refs_0_, f32[256,128]{1,0:T(8,128)S(1)} %get-tuple-element.71.refs_1_, f32[256,128]{1,0:T(8,128)S(1)} %get-tuple-element.72.refs_2_, ...), custom_call_target="tpu_custom_call" | custom-call | flops 393216 | bytes 2359296 | tf_op jit(solution)/shard_map/pack/pallas_call | solution.py:194
  99.5 4.3 %reflect_last.3 = (f32[512,128]{1,0:T(8,128)}, f32[1536,256]{1,0:T(8,128)}) custom-call(s32[1]{0:T(128)} %bitcast.panel, s32[1024]{0:T(1024)S(1)} %bitcast_add_fusion.slots, f32[512,128]{1,0:T(8,128)S(1)} %collective-permute-done.14.pivot, f32[4,256,512]{2,1,0:T(8,128)} %bitcast.53, bf16[4,256,512]{2,1,0:T(8,128)(2,1)S(1)} %get-tuple-element.46.vectors, ...), custom_call_target="tpu_custom_call" | custom-call | flops 268435456 | bytes 4718592 | tf_op jit(solution)/shard_map/reflect_last/pallas_call | solution.py:118
  103.7 10.4 %all-to-all-start = ((f32[64,24,256]{2,1,0:T(8,128)}), f32[64,24,256]{2,1,0:T(8,128)S(1)}, u32[]{:S(2)}, u32[]{:S(2)}) async-start(f32[64,24,256]{2,1,0:T(8,128)} %bitcast.66), calls=%async_computation | async-start | bytes 3145728 | tf_op jit(solution)/shard_map/all_to_all | solution.py:374
  114.4 3.2 %project.3 = (f32[128,256]{1,0:T(8,128)S(1)}, f32[128,256]{1,0:T(8,128)}, f32[128,256]{1,0:T(8,128)}, f32[128,256]{1,0:T(8,128)}) custom-call(s32[1]{0:T(128)} %bitcast.14.owner, bf16[1536,512]{1,0:T(8,128)(2,1)S(1)} %bitcast.30, f32[1536,256]{1,0:T(8,128)} %bitcast.20.rows), custom_call_target="tpu_custom_call" | custom-call | flops 805306368 | bytes 3670016 | tf_op jit(solution)/shard_map/project/pallas_call | solution.py:225
  117.6 3.2 %collective-permute-start.24 = (f32[128,256]{1,0:T(8,128)}, f32[128,256]{1,0:T(8,128)}, u32[]{:S(2)}, u32[]{:S(2)}) collective-permute-start(f32[128,256]{1,0:T(8,128)} %get-tuple-element.87), channel_id=1, source_target_pairs={{0,3},{1,0},{2,1},{3,2},{4,7},{5,4},{6,5},{7,6},{8,11},{9,8},{10,9... | collective-permute-start | bytes 393224 | tf_op jit(solution)/shard_map/ppermute | solution.py:18
  123.6 30.6 %all-to-all-done = f32[64,24,256]{2,1,0:T(8,128)S(1)} async-done(((f32[64,24,256]{2,1,0:T(8,128)}), f32[64,24,256]{2,1,0:T(8,128)S(1)}, u32[]{:S(2)}, u32[]{:S(2)}) %all-to-all-start) | async-done | bytes 1572896 | tf_op jit(solution)/shard_map/all_to_all | solution.py:374
  155.5 3.2 %collective-permute-start.18 = (f32[128,256]{1,0:T(8,128)S(1)}, f32[128,256]{1,0:T(8,128)S(1)}, u32[]{:S(2)}, u32[]{:S(2)}) collective-permute-start(f32[128,256]{1,0:T(8,128)S(1)} %get-tuple-element.82), channel_id=1, source_target_pairs={{0,3},{1,0},{2,1},{3,2},{4,7},{5,4},{6,5},{7,6},{8,11},{9,8},{10,9... | collective-permute-start | bytes 393224 | tf_op jit(solution)/shard_map/ppermute | solution.py:18
  164.1 8.7 %collective-permute-done.17 = f32[128,256]{1,0:T(8,128)S(1)} collective-permute-done((f32[128,256]{1,0:T(8,128)S(1)}, f32[128,256]{1,0:T(8,128)S(1)}, u32[]{:S(2)}, u32[]{:S(2)}) %collective-permute-start.17) | collective-permute-done | bytes 131104 | tf_op jit(solution)/shard_map/ppermute | solution.py:18
  174.5 3.9 %collective-permute-done.16 = f32[128,256]{1,0:T(8,128)S(1)} collective-permute-done((f32[128,256]{1,0:T(8,128)S(1)}, f32[128,256]{1,0:T(8,128)S(1)}, u32[]{:S(2)}, u32[]{:S(2)}) %collective-permute-start.16) | collective-permute-done | bytes 131104 | tf_op jit(solution)/shard_map/ppermute | solution.py:18
  180.5 2.3 %collective-permute-done.25.refs_1_ = f32[128,256]{1,0:T(8,128)S(1)} collective-permute-done((f32[128,256]{1,0:T(8,128)S(1)}, f32[128,256]{1,0:T(8,128)S(1)}, u32[]{:S(2)}, u32[]{:S(2)}) %collective-permute-start.25) | collective-permute-done | bytes 131104 | tf_op jit(solution)/shard_map/ppermute | solution.py:18
  185.3 4.8 %finish.2.refs_4_ = f32[1536,512]{1,0:T(8,128)} custom-call(s32[1]{0:T(128)} %bitcast.14.owner, bf16[512,512]{1,0:T(8,128)(2,1)S(1)} %bitcast.36, bf16[1536,512]{1,0:T(8,128)(2,1)S(1)} %bitcast.32, f32[1536,256]{1,0:T(8,128)} %bitcast.20.rows, f32[128,256]{1,0:T(8,128)S(1)} %add_add_fusion.refs_0_, f32[128,256]{1,0:T(8,128)S(1)} %collective-permute-done.25.refs_1_, ...), custom_call_target="tpu_custom_call" | custom-call | flops 1073741824 | bytes 5767168 | tf_op jit(solution)/shard_map/finish/pallas_call | solution.py:269
  190.1 3.2 %finish.3 = f32[1536,512]{1,0:T(8,128)} custom-call(s32[1]{0:T(128)} %bitcast.14.owner, bf16[512,512]{1,0:T(8,128)(2,1)S(1)} %bitcast.37, bf16[1536,512]{1,0:T(8,128)(2,1)S(1)} %bitcast.33, f32[1536,256]{1,0:T(8,128)S(1)} %bitcast.35, f32[128,256]{1,0:T(8,128)S(1)} %add_add_fusion.1.refs_0_, ...), custom_call_target="tpu_custom_call", output_to_operand_aliasing={{}: (8, {})} | custom-call | flops 1073741824 | bytes 5767168 | tf_op jit(solution)/shard_map/finish/pallas_call | solution.py:269
  (108 shorter events, 57.5 us)
Async XLA Ops:
  3.3 10.7 %collective-permute-start = (f32[512,128]{1,0:T(8,128)}, f32[512,128]{1,0:T(8,128)}, u32[]{:S(2)}, u32[]{:S(2)}) collective-permute-start(f32[512,128]{1,0:T(8,128)} %get-tuple-element.45), channel_id=1, source_target_pairs={{0,1},{1,2},{2,3},{3,0},{4,5},{5,6},{6,7},{7,4},{8,9},{9,10},{10,1... | collective-permute-start | bytes 786440 | tf_op jit(solution)/shard_map/ppermute | solution.py:18
  8.0 10.3 %collective-permute-start.4 = (f32[512,128]{1,0:T(8,128)}, f32[512,128]{1,0:T(8,128)S(1)}, u32[]{:S(2)}, u32[]{:S(2)}) collective-permute-start(f32[512,128]{1,0:T(8,128)} %get-tuple-element.52), channel_id=1, source_target_pairs={{0,1},{1,2},{2,3},{3,0},{4,5},{5,6},{6,7},{7,4},{8,9},{9,10},{10,1... | collective-permute-start | bytes 786440 | tf_op jit(solution)/shard_map/ppermute | solution.py:18
  16.3 9.4 %collective-permute-start.1 = (f32[512,128]{1,0:T(8,128)}, f32[512,128]{1,0:T(8,128)}, u32[]{:S(2)}, u32[]{:S(2)}) collective-permute-start(f32[512,128]{1,0:T(8,128)} %get-tuple-element.49), channel_id=1, source_target_pairs={{0,1},{1,2},{2,3},{3,0},{4,5},{5,6},{6,7},{7,4},{8,9},{9,10},{10,1... | collective-permute-start | bytes 786440 | tf_op jit(solution)/shard_map/ppermute | solution.py:18
  21.2 9.7 %collective-permute-start.5 = (f32[512,128]{1,0:T(8,128)}, f32[512,128]{1,0:T(8,128)S(1)}, u32[]{:S(2)}, u32[]{:S(2)}) collective-permute-start(f32[512,128]{1,0:T(8,128)} %get-tuple-element.53), channel_id=1, source_target_pairs={{0,1},{1,2},{2,3},{3,0},{4,5},{5,6},{6,7},{7,4},{8,9},{9,10},{10,1... | collective-permute-start | bytes 786440 | tf_op jit(solution)/shard_map/ppermute | solution.py:18
  32.7 9.4 %collective-permute-start.6 = (f32[512,128]{1,0:T(8,128)S(1)}, f32[512,128]{1,0:T(8,128)S(1)}, u32[]{:S(2)}, u32[]{:S(2)}) collective-permute-start(f32[512,128]{1,0:T(8,128)S(1)} %get-tuple-element.54), channel_id=1, source_target_pairs={{0,1},{1,2},{2,3},{3,0},{4,5},{5,6},{6,7},{7,4},{8,9},{9,10},{10,1... | collective-permute-start | bytes 786440 | tf_op jit(solution)/shard_map/ppermute | solution.py:18
  46.3 57.4 %all-to-all-start.1 = ((f32[64,24,256]{2,1,0:T(8,128)}), f32[64,24,256]{2,1,0:T(8,128)}, u32[]{:S(2)}, u32[]{:S(2)}) async-start(f32[64,24,256]{2,1,0:T(8,128)} %bitcast.65), calls=%async_computation.1 | async-start | bytes 3145728 | tf_op jit(solution)/shard_map/all_to_all | solution.py:374
  61.6 10.6 %collective-permute-start.8 = (f32[512,128]{1,0:T(8,128)S(1)}, f32[512,128]{1,0:T(8,128)S(1)}, u32[]{:S(2)}, u32[]{:S(2)}) collective-permute-start(f32[512,128]{1,0:T(8,128)S(1)} %get-tuple-element.63), channel_id=1, source_target_pairs={{0,1},{1,2},{2,3},{3,0},{4,5},{5,6},{6,7},{7,4},{8,9},{9,10},{10,1... | collective-permute-start | bytes 786440 | tf_op jit(solution)/shard_map/ppermute | solution.py:18
  63.6 14.0 %collective-permute-start.12 = (f32[512,128]{1,0:T(8,128)S(1)}, f32[512,128]{1,0:T(8,128)S(1)}, u32[]{:S(2)}, u32[]{:S(2)}) collective-permute-start(f32[512,128]{1,0:T(8,128)S(1)} %get-tuple-element.67), channel_id=1, source_target_pairs={{0,1},{1,2},{2,3},{3,0},{4,5},{5,6},{6,7},{7,4},{8,9},{9,10},{10,1... | collective-permute-start | bytes 786440 | tf_op jit(solution)/shard_map/ppermute | solution.py:18
  79.4 10.5 %collective-permute-start.13 = (f32[512,128]{1,0:T(8,128)S(1)}, f32[512,128]{1,0:T(8,128)S(1)}, u32[]{:S(2)}, u32[]{:S(2)}) collective-permute-start(f32[512,128]{1,0:T(8,128)S(1)} %get-tuple-element.68), channel_id=1, source_target_pairs={{0,1},{1,2},{2,3},{3,0},{4,5},{5,6},{6,7},{7,4},{8,9},{9,10},{10,1... | collective-permute-start | bytes 786440 | tf_op jit(solution)/shard_map/ppermute | solution.py:18
  85.0 10.3 %collective-permute-start.10 = (f32[512,128]{1,0:T(8,128)S(1)}, f32[512,128]{1,0:T(8,128)S(1)}, u32[]{:S(2)}, u32[]{:S(2)}) collective-permute-start(f32[512,128]{1,0:T(8,128)S(1)} %get-tuple-element.65), channel_id=1, source_target_pairs={{0,1},{1,2},{2,3},{3,0},{4,5},{5,6},{6,7},{7,4},{8,9},{9,10},{10,1... | collective-permute-start | bytes 786440 | tf_op jit(solution)/shard_map/ppermute | solution.py:18
  103.7 50.4 %all-to-all-start = ((f32[64,24,256]{2,1,0:T(8,128)}), f32[64,24,256]{2,1,0:T(8,128)S(1)}, u32[]{:S(2)}, u32[]{:S(2)}) async-start(f32[64,24,256]{2,1,0:T(8,128)} %bitcast.66), calls=%async_computation | async-start | bytes 3145728 | tf_op jit(solution)/shard_map/all_to_all | solution.py:374
  114.2 41.1 %collective-permute-start.3 = (f32[512,128]{1,0:T(8,128)}, f32[512,128]{1,0:T(8,128)S(1)}, u32[]{:S(2)}, u32[]{:S(2)}) collective-permute-start(f32[512,128]{1,0:T(8,128)} %copy-done.13), channel_id=1, source_target_pairs={{0,1},{1,2},{2,3},{3,0},{4,5},{5,6},{6,7},{7,4},{8,9},{9,10},{10,1... | collective-permute-start | bytes 786440 | tf_op jit(solution)/shard_map/ppermute | solution.py:18
  114.2 41.1 %collective-permute-start.7 = (f32[512,128]{1,0:T(8,128)}, f32[512,128]{1,0:T(8,128)}, u32[]{:S(2)}, u32[]{:S(2)}) collective-permute-start(f32[512,128]{1,0:T(8,128)} %get-tuple-element.62), channel_id=1, source_target_pairs={{0,1},{1,2},{2,3},{3,0},{4,5},{5,6},{6,7},{7,4},{8,9},{9,10},{10,1... | collective-permute-start | bytes 786440 | tf_op jit(solution)/shard_map/ppermute | solution.py:18
  117.6 37.9 %collective-permute-start.24 = (f32[128,256]{1,0:T(8,128)}, f32[128,256]{1,0:T(8,128)}, u32[]{:S(2)}, u32[]{:S(2)}) collective-permute-start(f32[128,256]{1,0:T(8,128)} %get-tuple-element.87), channel_id=1, source_target_pairs={{0,3},{1,0},{2,1},{3,2},{4,7},{5,4},{6,5},{7,6},{8,11},{9,8},{10,9... | collective-permute-start | bytes 393224 | tf_op jit(solution)/shard_map/ppermute | solution.py:18
  120.8 37.9 %collective-permute-start.23 = (f32[128,256]{1,0:T(8,128)}, f32[128,256]{1,0:T(8,128)}, u32[]{:S(2)}, u32[]{:S(2)}) collective-permute-start(f32[128,256]{1,0:T(8,128)} %get-tuple-element.86), channel_id=1, source_target_pairs={{0,2},{1,3},{2,0},{3,1},{4,6},{5,7},{6,4},{7,5},{8,10},{9,11},{10,... | collective-permute-start | bytes 393224 | tf_op jit(solution)/shard_map/ppermute | solution.py:18
  122.2 38.0 %collective-permute-start.22 = (f32[128,256]{1,0:T(8,128)}, f32[128,256]{1,0:T(8,128)}, u32[]{:S(2)}, u32[]{:S(2)}) collective-permute-start(f32[128,256]{1,0:T(8,128)} %get-tuple-element.85), channel_id=1, source_target_pairs={{0,1},{1,2},{2,3},{3,0},{4,5},{5,6},{6,7},{7,4},{8,9},{9,10},{10,1... | collective-permute-start | bytes 393224 | tf_op jit(solution)/shard_map/ppermute | solution.py:18
  155.3 23.2 %collective-permute-start.11 = (f32[512,128]{1,0:T(8,128)S(1)}, f32[512,128]{1,0:T(8,128)S(1)}, u32[]{:S(2)}, u32[]{:S(2)}) collective-permute-start(f32[512,128]{1,0:T(8,128)S(1)} %copy-done.15), channel_id=1, source_target_pairs={{0,1},{1,2},{2,3},{3,0},{4,5},{5,6},{6,7},{7,4},{8,9},{9,10},{10,1... | collective-permute-start | bytes 786440 | tf_op jit(solution)/shard_map/ppermute | solution.py:18
  155.4 25.2 %collective-permute-start.15 = (f32[512,128]{1,0:T(8,128)S(1)}, f32[512,128]{1,0:T(8,128)S(1)}, u32[]{:S(2)}, u32[]{:S(2)}) collective-permute-start(f32[512,128]{1,0:T(8,128)S(1)} %copy-done.17), channel_id=1, source_target_pairs={{0,1},{1,2},{2,3},{3,0},{4,5},{5,6},{6,7},{7,4},{8,9},{9,10},{10,1... | collective-permute-start | bytes 786440 | tf_op jit(solution)/shard_map/ppermute | solution.py:18
  158.7 14.1 %collective-permute-start.17 = (f32[128,256]{1,0:T(8,128)S(1)}, f32[128,256]{1,0:T(8,128)S(1)}, u32[]{:S(2)}, u32[]{:S(2)}) collective-permute-start(f32[128,256]{1,0:T(8,128)S(1)} %get-tuple-element.81), channel_id=1, source_target_pairs={{0,2},{1,3},{2,0},{3,1},{4,6},{5,7},{6,4},{7,5},{8,10},{9,11},{10,... | collective-permute-start | bytes 393224 | tf_op jit(solution)/shard_map/ppermute | solution.py:18
  160.1 18.2 %collective-permute-start.16 = (f32[128,256]{1,0:T(8,128)S(1)}, f32[128,256]{1,0:T(8,128)S(1)}, u32[]{:S(2)}, u32[]{:S(2)}) collective-permute-start(f32[128,256]{1,0:T(8,128)S(1)} %get-tuple-element.80), channel_id=1, source_target_pairs={{0,1},{1,2},{2,3},{3,0},{4,5},{5,6},{6,7},{7,4},{8,9},{9,10},{10,1... | collective-permute-start | bytes 393224 | tf_op jit(solution)/shard_map/ppermute | solution.py:18
  162.6 20.2 %collective-permute-start.25 = (f32[128,256]{1,0:T(8,128)S(1)}, f32[128,256]{1,0:T(8,128)S(1)}, u32[]{:S(2)}, u32[]{:S(2)}) collective-permute-start(f32[128,256]{1,0:T(8,128)S(1)} %add_add_fusion.refs_0_), channel_id=1, source_target_pairs={{0,1},{1,2},{2,3},{3,0},{4,5},{5,6},{6,7},{7,4},{8,9},{9,10},{10,1... | collective-permute-start | bytes 393224 | tf_op jit(solution)/shard_map/ppermute | solution.py:18
  172.8 12.5 %collective-permute-start.26 = (f32[128,256]{1,0:T(8,128)S(1)}, f32[128,256]{1,0:T(8,128)S(1)}, u32[]{:S(2)}, u32[]{:S(2)}) collective-permute-start(f32[128,256]{1,0:T(8,128)S(1)} %add_add_fusion.refs_0_), channel_id=1, source_target_pairs={{0,2},{1,3},{2,0},{3,1},{4,6},{5,7},{6,4},{7,5},{8,10},{9,11},{10,... | collective-permute-start | bytes 393224 | tf_op jit(solution)/shard_map/ppermute | solution.py:18
  178.4 11.6 %collective-permute-start.19 = (f32[128,256]{1,0:T(8,128)S(1)}, f32[128,256]{1,0:T(8,128)S(1)}, u32[]{:S(2)}, u32[]{:S(2)}) collective-permute-start(f32[128,256]{1,0:T(8,128)S(1)} %add_add_fusion.1.refs_0_), channel_id=1, source_target_pairs={{0,1},{1,2},{2,3},{3,0},{4,5},{5,6},{6,7},{7,4},{8,9},{9,10},{10,1... | collective-permute-start | bytes 393224 | tf_op jit(solution)/shard_map/ppermute | solution.py:18
  180.5 9.5 %collective-permute-start.20 = (f32[128,256]{1,0:T(8,128)S(1)}, f32[128,256]{1,0:T(8,128)S(1)}, u32[]{:S(2)}, u32[]{:S(2)}) collective-permute-start(f32[128,256]{1,0:T(8,128)S(1)} %add_add_fusion.1.refs_0_), channel_id=1, source_target_pairs={{0,2},{1,3},{2,0},{3,1},{4,6},{5,7},{6,4},{7,5},{8,10},{9,11},{10,... | collective-permute-start | bytes 393224 | tf_op jit(solution)/shard_map/ppermute | solution.py:18
  (25 other events, 138.1 us)
where the time goes:
time: 195 us; the launch traced here: 193 us
  waiting for transfers between devices  78.7 us (40%)
  Pallas kernels  58.6 us (30%)
  starting transfers between devices  48.2 us (25%)
  local copies, waits for them, and re-layouts  4.5 us (2%)
    ppermute x28, waiting for transfers between devices, passed_along(): return lax.ppermute(value, 'sect', pairs)  48.1 us
    all_to_all x2, waiting for transfers between devices, local(): lax.all_to_all(packed.reshape(owners, capacity, width), 'front', split_ax...  30.6 us
    pallas_call x14, Pallas kernels, reflect(): pl.pallas_call(body, grid_spec=pltpu.PrefetchScalarGridSpec(num_scalar_pr...  27 us
    ppermute x28, starting transfers between devices, passed_along(): return lax.ppermute(value, 'sect', pairs)  25.5 us
    all_to_all x2, starting transfers between devices, local(): lax.all_to_all(packed.reshape(owners, capacity, width), 'front', split_ax...  22.7 us
    pallas_call x2, Pallas kernels, reflect_last(): pl.pallas_call(functools.partial(last_kernel, step), grid_spec=pltpu.Pref...  8.52 us
    pallas_call x2, Pallas kernels, finish(): pl.pallas_call(functools.partial(finish_kernel, len(parts)), grid_spec=pl...  8.01 us
    pallas_call x2, Pallas kernels, pack(): pl.pallas_call(functools.partial(pack_kernel, len(streams[0])), grid_spec...  5.15 us
  transfers between devices with their start and end apart: 30, of which 16 were waited for; matrix products, arithmetic and copies ran while one was open for 1% of the time, Pallas kernels for 25%

commit v1 on v0

--- a/solution.py
+++ b/solution.py
@@ -45,9 +45,10 @@
 
 
 def reflect_kernel(step, panel, pivot, block, vectors, turned, factor, pivot_out, block_out):
-    change = product(factor[step], pivot[...] + product(turned[step], block[0], 1), 1)
+    at = step - 1
+    change = product(factor[at], pivot[...] + product(turned[at], block[0], 1), 1)
     pivot_out[...] = pivot[...] - change
-    block_out[...] = block[0] - product(vectors[step], change, 1)
+    block_out[...] = block[0] - product(vectors[at], change, 1)
 
 
 def place_rows(slots, base, blocks, out):
@@ -98,7 +99,7 @@
         ),
         out_shape=[
             jax.ShapeDtypeStruct((size, width), jnp.float32),
-            jax.ShapeDtypeStruct((rows, width), jnp.float32),
+            pltpu.VMEM((rows, width), jnp.float32),
         ],
         cost_estimate=pl.CostEstimate(
             flops=4 * width * size * (2 * rows + size),
@@ -124,7 +125,7 @@
                 pl.BlockSpec((size, width), lambda i, p, s: (0, 0)),
                 pl.BlockSpec((1, rows, width), lambda i, p, s: (p[0], 0, at)),
                 *[pl.BlockSpec(memory_space=pltpu.VMEM)] * 3,
-                pl.BlockSpec((total, wide), lambda i, p, s: (0, 0)),
+                pl.BlockSpec(memory_space=pltpu.VMEM),
                 *[pl.BlockSpec(other.shape, lambda i, p, s: (0, 0)) for other in others],
             ],
             out_specs=[
@@ -155,7 +156,8 @@
 
 
 def stage(panels, vectors, factors):
-    count, rows, size = vectors.shape
+    rows, size = vectors.shape[1:]
+    count = panels.shape[0]
     whole = pl.BlockSpec(memory_space=pltpu.VMEM)
     return pl.pallas_call(
         stage_kernel,
@@ -197,9 +199,9 @@
             num_scalar_prefetch=2,
             grid=(1,),
             in_specs=[pl.BlockSpec(b.shape, lambda i, *_: (0, 0)) for b in blocks],
-            out_specs=pl.BlockSpec((total, wide), lambda i, *_: (0, 0)),
-        ),
-        out_shape=jax.ShapeDtypeStruct((total, wide), jnp.float32),
+            out_specs=pl.BlockSpec(memory_space=pltpu.VMEM),
+        ),
+        out_shape=pltpu.VMEM((total, wide), jnp.float32),
         cost_estimate=pl.CostEstimate(
             flops=total * wide, bytes_accessed=6 * wide * total, transcendentals=0
         ),
@@ -339,15 +341,15 @@
     bases = jnp.concatenate(panel_at) * rows
     owner = me.astype(jnp.int32)[None]
     vectors, factor = parent_vectors[0, 0], parent_factor[0]
-    weights = stage(jnp.concatenate(panel_at), sect_vectors, sect_factors)
+    weights = stage(jnp.concatenate(panel_at[1:]), sect_vectors, sect_factors)
     tops, out = [], None
-    for chunk, streams in enumerate(CHUNKS):
+    for streams in CHUNKS:
         column, width = streams[0][0], sum(width for _, width in streams)
         updated, moving = [], []
         for first, narrow in streams:
             pivot, blocks = pivots, []
             for step in range(count - 1):
-                direct = chunk == 0 and step == 0
+                direct = step == 0
                 pivot, block = reflect(
                     panel_at[step], step, pivot, first, narrow, sections,
                     (sect_vectors, sect_factors) if direct else weights,

time: 195 us -> 193 us (0.990)
  local copies, waits for them, and re-layouts: 4.5 us -> 1.38 us
  waiting for transfers between devices: 78.7 us -> 81.1 us
    unnamed x38 -> x18, local copies, waits for them, and re-layouts: 4.5 us -> 1.38 us
    ppermute x28, waiting for transfers between devices: 48.1 us -> 50.5 us  [passed_along(): return lax.ppermute(value, 'sect', pairs)]
where the time goes in v1:
time: 193 us; the launch traced here: 191 us
  waiting for transfers between devices  81.1 us (42%)
  Pallas kernels  57.7 us (30%)
  starting transfers between devices  48.2 us (25%)
    ppermute x28, waiting for transfers between devices, passed_along(): return lax.ppermute(value, 'sect', pairs)  50.5 us
    all_to_all x2, waiting for transfers between devices, local(): lax.all_to_all(packed.reshape(owners, capacity, width), 'front', split_ax...  30.6 us
    pallas_call x14, Pallas kernels, reflect(): pl.pallas_call(body, grid_spec=pltpu.PrefetchScalarGridSpec(num_scalar_pr...  26.5 us
    ppermute x28, starting transfers between devices, passed_along(): return lax.ppermute(value, 'sect', pairs)  25.5 us
    all_to_all x2, starting transfers between devices, local(): lax.all_to_all(packed.reshape(owners, capacity, width), 'front', split_ax...  22.7 us
    pallas_call x2, Pallas kernels, reflect_last(): pl.pallas_call(functools.partial(last_kernel, step), grid_spec=pltpu.Pref...  8.54 us
    pallas_call x2, Pallas kernels, finish(): pl.pallas_call(functools.partial(finish_kernel, len(parts)), grid_spec=pl...  8 us
    pallas_call x2, Pallas kernels, pack(): pl.pallas_call(functools.partial(pack_kernel, len(streams[0])), grid_spec...  5.15 us
  transfers between devices with their start and end apart: 30, of which 16 were waited for; matrix products, arithmetic and copies ran while one was open for 1% of the time, Pallas kernels for 25%

profile of v1, /device:TPU:8, one launch (start us, length us, event | category | flops | bytes accessed | tf_op | source)
XLA Modules:
  0.0 191.2 jit_solution(10667217334569824018)
XLA Ops:
  0.6 2.6 %reflect.14 = (f32[512,128]{1,0:T(8,128)}, f32[256,128]{1,0:T(8,128)S(1)}) custom-call(s32[1]{0:T(128)} %bitcast.3.panel, f32[512,512]{1,0:T(8,128)} %bitcast.64, f32[4,256,512]{2,1,0:T(8,128)} %bitcast.38, bf16[4,256,512]{2,1,0:T(8,128)(2,1)} %bitcast.59, bf16[4,512,512]{2,1,0:T(8,128)(2,1)} %bitcast.54), custom_call_target="tpu_custom_call" | custom-call | flops 268435456 | bytes 1572864 | tf_op jit(solution)/shard_map/reflect/pallas_call | solution.py:85
  4.8 2.6 %reflect.18 = (f32[512,128]{1,0:T(8,128)}, f32[256,128]{1,0:T(8,128)S(1)}) custom-call(s32[1]{0:T(128)} %bitcast.3.panel, f32[512,512]{1,0:T(8,128)} %bitcast.65, f32[4,256,512]{2,1,0:T(8,128)} %bitcast.39, bf16[4,256,512]{2,1,0:T(8,128)(2,1)} %bitcast.60, bf16[4,512,512]{2,1,0:T(8,128)(2,1)} %bitcast.55), custom_call_target="tpu_custom_call" | custom-call | flops 268435456 | bytes 1572864 | tf_op jit(solution)/shard_map/reflect/pallas_call | solution.py:85
  9.6 3.4 %stage.1 = (bf16[3,256,512]{2,1,0:T(8,128)(2,1)S(1)}, bf16[3,512,256]{2,1,0:T(8,128)(2,1)S(1)}, bf16[3,512,512]{2,1,0:T(8,128)(2,1)S(1)}) custom-call(s32[3]{0:T(128)S(1)} %pad_add_fusion.panels, bf16[4,256,512]{2,1,0:T(8,128)(2,1)} %bitcast.61, bf16[4,512,512]{2,1,0:T(8,128)(2,1)} %bitcast.56), custom_call_target="tpu_custom_call" | custom-call | bytes 2359296 | tf_op jit(solution)/shard_map/stage/pallas_call | solution.py:162
  21.2 3.8 %collective-permute-done.1.pivot = f32[512,128]{1,0:T(8,128)S(1)} collective-permute-done((f32[512,128]{1,0:T(8,128)S(1)}, f32[512,128]{1,0:T(8,128)S(1)}, u32[]{:S(2)}, u32[]{:S(2)}) %collective-permute-start.1) | collective-permute-done | bytes 262176 | tf_op jit(solution)/shard_map/ppermute | solution.py:18
  27.2 3.6 %collective-permute-done.5.pivot = f32[512,128]{1,0:T(8,128)S(1)} collective-permute-done((f32[512,128]{1,0:T(8,128)S(1)}, f32[512,128]{1,0:T(8,128)S(1)}, u32[]{:S(2)}, u32[]{:S(2)}) %collective-permute-start.5) | collective-permute-done | bytes 262176 | tf_op jit(solution)/shard_map/ppermute | solution.py:18
  32.9 2.6 %pack.2.packed = f32[1536,256]{1,0:T(8,128)S(1)} custom-call(s32[4]{0:T(128)S(1)} %add_multiply_fusion.bases, s32[1024]{0:T(1024)S(1)} %bitcast_add_fusion.slots, f32[256,128]{1,0:T(8,128)S(1)} %get-tuple-element.55.refs_0_, f32[256,128]{1,0:T(8,128)S(1)} %get-tuple-element.56.refs_1_, f32[256,128]{1,0:T(8,128)S(1)} %get-tuple-element.57.refs_2_, ...), custom_call_target="tpu_custom_call" | custom-call | flops 393216 | bytes 2359296 | tf_op jit(solution)/shard_map/pack/pallas_call | solution.py:196
  38.0 2.8 %collective-permute-done.6.pivot = f32[512,128]{1,0:T(8,128)S(1)} collective-permute-done((f32[512,128]{1,0:T(8,128)S(1)}, f32[512,128]{1,0:T(8,128)S(1)}, u32[]{:S(2)}, u32[]{:S(2)}) %collective-permute-start.6) | collective-permute-done | bytes 262176 | tf_op jit(solution)/shard_map/ppermute | solution.py:18
  40.8 4.3 %reflect_last.2 = (f32[512,128]{1,0:T(8,128)}, f32[1536,256]{1,0:T(8,128)}) custom-call(s32[1]{0:T(128)} %bitcast.panel, s32[1024]{0:T(1024)S(1)} %bitcast_add_fusion.slots, f32[512,128]{1,0:T(8,128)S(1)} %collective-permute-done.6.pivot, f32[4,256,512]{2,1,0:T(8,128)} %bitcast.45, bf16[3,256,512]{2,1,0:T(8,128)(2,1)S(1)} %get-tuple-element.46.vectors, ...), custom_call_target="tpu_custom_call" | custom-call | flops 268435456 | bytes 4718592 | tf_op jit(solution)/shard_map/reflect_last/pallas_call | solution.py:119
  45.1 12.3 %all-to-all-start.1 = ((f32[64,24,256]{2,1,0:T(8,128)}), f32[64,24,256]{2,1,0:T(8,128)}, u32[]{:S(2)}, u32[]{:S(2)}) async-start(f32[64,24,256]{2,1,0:T(8,128)} %bitcast.69), calls=%async_computation.1 | async-start | bytes 3145728 | tf_op jit(solution)/shard_map/all_to_all | solution.py:376
  63.7 6.4 %collective-permute-done.8.pivot = f32[512,128]{1,0:T(8,128)S(1)} collective-permute-done((f32[512,128]{1,0:T(8,128)S(1)}, f32[512,128]{1,0:T(8,128)S(1)}, u32[]{:S(2)}, u32[]{:S(2)}) %collective-permute-start.8) | collective-permute-done | bytes 262176 | tf_op jit(solution)/shard_map/ppermute | solution.py:18
  71.9 3.6 %collective-permute-done.12.pivot = f32[512,128]{1,0:T(8,128)S(1)} collective-permute-done((f32[512,128]{1,0:T(8,128)S(1)}, f32[512,128]{1,0:T(8,128)S(1)}, u32[]{:S(2)}, u32[]{:S(2)}) %collective-permute-start.12) | collective-permute-done | bytes 262176 | tf_op jit(solution)/shard_map/ppermute | solution.py:18
  77.3 3.8 %collective-permute-done.9.pivot = f32[512,128]{1,0:T(8,128)S(1)} collective-permute-done((f32[512,128]{1,0:T(8,128)S(1)}, f32[512,128]{1,0:T(8,128)S(1)}, u32[]{:S(2)}, u32[]{:S(2)}) %collective-permute-start.9) | collective-permute-done | bytes 262176 | tf_op jit(solution)/shard_map/ppermute | solution.py:18
  83.0 4.8 %collective-permute-done.13.pivot = f32[512,128]{1,0:T(8,128)S(1)} collective-permute-done((f32[512,128]{1,0:T(8,128)S(1)}, f32[512,128]{1,0:T(8,128)S(1)}, u32[]{:S(2)}, u32[]{:S(2)}) %collective-permute-start.13) | collective-permute-done | bytes 262176 | tf_op jit(solution)/shard_map/ppermute | solution.py:18
  89.5 2.6 %pack.3.packed = f32[1536,256]{1,0:T(8,128)S(1)} custom-call(s32[4]{0:T(128)S(1)} %add_multiply_fusion.bases, s32[1024]{0:T(1024)S(1)} %bitcast_add_fusion.slots, f32[256,128]{1,0:T(8,128)S(1)} %get-tuple-element.70.refs_0_, f32[256,128]{1,0:T(8,128)S(1)} %get-tuple-element.71.refs_1_, f32[256,128]{1,0:T(8,128)S(1)} %get-tuple-element.72.refs_2_, ...), custom_call_target="tpu_custom_call" | custom-call | flops 393216 | bytes 2359296 | tf_op jit(solution)/shard_map/pack/pallas_call | solution.py:196
  97.4 4.3 %reflect_last.3 = (f32[512,128]{1,0:T(8,128)}, f32[1536,256]{1,0:T(8,128)}) custom-call(s32[1]{0:T(128)} %bitcast.panel, s32[1024]{0:T(1024)S(1)} %bitcast_add_fusion.slots, f32[512,128]{1,0:T(8,128)S(1)} %collective-permute-done.14.pivot, f32[4,256,512]{2,1,0:T(8,128)} %bitcast.53, bf16[3,256,512]{2,1,0:T(8,128)(2,1)S(1)} %get-tuple-element.46.vectors, ...), custom_call_target="tpu_custom_call" | custom-call | flops 268435456 | bytes 4718592 | tf_op jit(solution)/shard_map/reflect_last/pallas_call | solution.py:119
  101.6 10.4 %all-to-all-start = ((f32[64,24,256]{2,1,0:T(8,128)}), f32[64,24,256]{2,1,0:T(8,128)S(1)}, u32[]{:S(2)}, u32[]{:S(2)}) async-start(f32[64,24,256]{2,1,0:T(8,128)} %bitcast.70), calls=%async_computation | async-start | bytes 3145728 | tf_op jit(solution)/shard_map/all_to_all | solution.py:376
  112.7 3.2 %project.3 = (f32[128,256]{1,0:T(8,128)S(1)}, f32[128,256]{1,0:T(8,128)}, f32[128,256]{1,0:T(8,128)}, f32[128,256]{1,0:T(8,128)}) custom-call(s32[1]{0:T(128)} %bitcast.14.owner, bf16[1536,512]{1,0:T(8,128)(2,1)S(1)} %bitcast.30, f32[1536,256]{1,0:T(8,128)} %bitcast.20.rows), custom_call_target="tpu_custom_call" | custom-call | flops 805306368 | bytes 3670016 | tf_op jit(solution)/shard_map/project/pallas_call | solution.py:227
  115.9 2.8 %collective-permute-start.24 = (f32[128,256]{1,0:T(8,128)}, f32[128,256]{1,0:T(8,128)}, u32[]{:S(2)}, u32[]{:S(2)}) collective-permute-start(f32[128,256]{1,0:T(8,128)} %get-tuple-element.87), channel_id=1, source_target_pairs={{0,3},{1,0},{2,1},{3,2},{4,7},{5,4},{6,5},{7,6},{8,11},{9,8},{10,9... | collective-permute-start | bytes 393224 | tf_op jit(solution)/shard_map/ppermute | solution.py:18
  121.5 30.6 %all-to-all-done = f32[64,24,256]{2,1,0:T(8,128)S(1)} async-done(((f32[64,24,256]{2,1,0:T(8,128)}), f32[64,24,256]{2,1,0:T(8,128)S(1)}, u32[]{:S(2)}, u32[]{:S(2)}) %all-to-all-start) | async-done | bytes 1572896 | tf_op jit(solution)/shard_map/all_to_all | solution.py:376
  153.8 2.8 %collective-permute-start.18 = (f32[128,256]{1,0:T(8,128)S(1)}, f32[128,256]{1,0:T(8,128)S(1)}, u32[]{:S(2)}, u32[]{:S(2)}) collective-permute-start(f32[128,256]{1,0:T(8,128)S(1)} %get-tuple-element.82), channel_id=1, source_target_pairs={{0,3},{1,0},{2,1},{3,2},{4,7},{5,4},{6,5},{7,6},{8,11},{9,8},{10,9... | collective-permute-start | bytes 393224 | tf_op jit(solution)/shard_map/ppermute | solution.py:18
  162.0 8.7 %collective-permute-done.17 = f32[128,256]{1,0:T(8,128)S(1)} collective-permute-done((f32[128,256]{1,0:T(8,128)S(1)}, f32[128,256]{1,0:T(8,128)S(1)}, u32[]{:S(2)}, u32[]{:S(2)}) %collective-permute-start.17) | collective-permute-done | bytes 131104 | tf_op jit(solution)/shard_map/ppermute | solution.py:18
  172.4 3.9 %collective-permute-done.16 = f32[128,256]{1,0:T(8,128)S(1)} collective-permute-done((f32[128,256]{1,0:T(8,128)S(1)}, f32[128,256]{1,0:T(8,128)S(1)}, u32[]{:S(2)}, u32[]{:S(2)}) %collective-permute-start.16) | collective-permute-done | bytes 131104 | tf_op jit(solution)/shard_map/ppermute | solution.py:18
  183.2 4.8 %finish.2.refs_4_ = f32[1536,512]{1,0:T(8,128)} custom-call(s32[1]{0:T(128)} %bitcast.14.owner, bf16[512,512]{1,0:T(8,128)(2,1)S(1)} %bitcast.36, bf16[1536,512]{1,0:T(8,128)(2,1)S(1)} %bitcast.32, f32[1536,256]{1,0:T(8,128)} %bitcast.20.rows, f32[128,256]{1,0:T(8,128)S(1)} %add_add_fusion.refs_0_, f32[128,256]{1,0:T(8,128)S(1)} %collective-permute-done.25.refs_1_, ...), custom_call_target="tpu_custom_call" | custom-call | flops 1073741824 | bytes 5767168 | tf_op jit(solution)/shard_map/finish/pallas_call | solution.py:271
  188.0 3.2 %finish.3 = f32[1536,512]{1,0:T(8,128)} custom-call(s32[1]{0:T(128)} %bitcast.14.owner, bf16[512,512]{1,0:T(8,128)(2,1)S(1)} %bitcast.37, bf16[1536,512]{1,0:T(8,128)(2,1)S(1)} %bitcast.33, f32[1536,256]{1,0:T(8,128)S(1)} %bitcast.35, f32[128,256]{1,0:T(8,128)S(1)} %add_add_fusion.1.refs_0_, ...), custom_call_target="tpu_custom_call", output_to_operand_aliasing={{}: (8, {})} | custom-call | flops 1073741824 | bytes 5767168 | tf_op jit(solution)/shard_map/finish/pallas_call | solution.py:271
  (89 shorter events, 56.5 us)
Async XLA Ops:
  3.3 10.7 %collective-permute-start = (f32[512,128]{1,0:T(8,128)}, f32[512,128]{1,0:T(8,128)}, u32[]{:S(2)}, u32[]{:S(2)}) collective-permute-start(f32[512,128]{1,0:T(8,128)} %get-tuple-element.45), channel_id=1, source_target_pairs={{0,1},{1,2},{2,3},{3,0},{4,5},{5,6},{6,7},{7,4},{8,9},{9,10},{10,1... | collective-permute-start | bytes 786440 | tf_op jit(solution)/shard_map/ppermute | solution.py:18
  8.0 10.6 %collective-permute-start.4 = (f32[512,128]{1,0:T(8,128)}, f32[512,128]{1,0:T(8,128)S(1)}, u32[]{:S(2)}, u32[]{:S(2)}) collective-permute-start(f32[512,128]{1,0:T(8,128)} %get-tuple-element.52), channel_id=1, source_target_pairs={{0,1},{1,2},{2,3},{3,0},{4,5},{5,6},{6,7},{7,4},{8,9},{9,10},{10,1... | collective-permute-start | bytes 786440 | tf_op jit(solution)/shard_map/ppermute | solution.py:18
  20.3 10.5 %collective-permute-start.5 = (f32[512,128]{1,0:T(8,128)S(1)}, f32[512,128]{1,0:T(8,128)S(1)}, u32[]{:S(2)}, u32[]{:S(2)}) collective-permute-start(f32[512,128]{1,0:T(8,128)S(1)} %get-tuple-element.53), channel_id=1, source_target_pairs={{0,1},{1,2},{2,3},{3,0},{4,5},{5,6},{6,7},{7,4},{8,9},{9,10},{10,1... | collective-permute-start | bytes 786440 | tf_op jit(solution)/shard_map/ppermute | solution.py:18
  26.7 9.6 %collective-permute-start.2 = (f32[512,128]{1,0:T(8,128)S(1)}, f32[512,128]{1,0:T(8,128)S(1)}, u32[]{:S(2)}, u32[]{:S(2)}) collective-permute-start(f32[512,128]{1,0:T(8,128)S(1)} %get-tuple-element.50), channel_id=1, source_target_pairs={{0,1},{1,2},{2,3},{3,0},{4,5},{5,6},{6,7},{7,4},{8,9},{9,10},{10,1... | collective-permute-start | bytes 786440 | tf_op jit(solution)/shard_map/ppermute | solution.py:18
  45.1 56.5 %all-to-all-start.1 = ((f32[64,24,256]{2,1,0:T(8,128)}), f32[64,24,256]{2,1,0:T(8,128)}, u32[]{:S(2)}, u32[]{:S(2)}) async-start(f32[64,24,256]{2,1,0:T(8,128)} %bitcast.69), calls=%async_computation.1 | async-start | bytes 3145728 | tf_op jit(solution)/shard_map/all_to_all | solution.py:376
  59.5 10.6 %collective-permute-start.8 = (f32[512,128]{1,0:T(8,128)S(1)}, f32[512,128]{1,0:T(8,128)S(1)}, u32[]{:S(2)}, u32[]{:S(2)}) collective-permute-start(f32[512,128]{1,0:T(8,128)S(1)} %get-tuple-element.63), channel_id=1, source_target_pairs={{0,1},{1,2},{2,3},{3,0},{4,5},{5,6},{6,7},{7,4},{8,9},{9,10},{10,1... | collective-permute-start | bytes 786440 | tf_op jit(solution)/shard_map/ppermute | solution.py:18
  62.1 13.4 %collective-permute-start.12 = (f32[512,128]{1,0:T(8,128)S(1)}, f32[512,128]{1,0:T(8,128)S(1)}, u32[]{:S(2)}, u32[]{:S(2)}) collective-permute-start(f32[512,128]{1,0:T(8,128)S(1)} %get-tuple-element.67), channel_id=1, source_target_pairs={{0,1},{1,2},{2,3},{3,0},{4,5},{5,6},{6,7},{7,4},{8,9},{9,10},{10,1... | collective-permute-start | bytes 786440 | tf_op jit(solution)/shard_map/ppermute | solution.py:18
  71.8 9.3 %collective-permute-start.9 = (f32[512,128]{1,0:T(8,128)S(1)}, f32[512,128]{1,0:T(8,128)S(1)}, u32[]{:S(2)}, u32[]{:S(2)}) collective-permute-start(f32[512,128]{1,0:T(8,128)S(1)} %get-tuple-element.64), channel_id=1, source_target_pairs={{0,1},{1,2},{2,3},{3,0},{4,5},{5,6},{6,7},{7,4},{8,9},{9,10},{10,1... | collective-permute-start | bytes 786440 | tf_op jit(solution)/shard_map/ppermute | solution.py:18
  77.3 10.5 %collective-permute-start.13 = (f32[512,128]{1,0:T(8,128)S(1)}, f32[512,128]{1,0:T(8,128)S(1)}, u32[]{:S(2)}, u32[]{:S(2)}) collective-permute-start(f32[512,128]{1,0:T(8,128)S(1)} %get-tuple-element.68), channel_id=1, source_target_pairs={{0,1},{1,2},{2,3},{3,0},{4,5},{5,6},{6,7},{7,4},{8,9},{9,10},{10,1... | collective-permute-start | bytes 786440 | tf_op jit(solution)/shard_map/ppermute | solution.py:18
  82.9 10.3 %collective-permute-start.10 = (f32[512,128]{1,0:T(8,128)S(1)}, f32[512,128]{1,0:T(8,128)S(1)}, u32[]{:S(2)}, u32[]{:S(2)}) collective-permute-start(f32[512,128]{1,0:T(8,128)S(1)} %get-tuple-element.65), channel_id=1, source_target_pairs={{0,1},{1,2},{2,3},{3,0},{4,5},{5,6},{6,7},{7,4},{8,9},{9,10},{10,1... | collective-permute-start | bytes 786440 | tf_op jit(solution)/shard_map/ppermute | solution.py:18
  101.6 50.4 %all-to-all-start = ((f32[64,24,256]{2,1,0:T(8,128)}), f32[64,24,256]{2,1,0:T(8,128)S(1)}, u32[]{:S(2)}, u32[]{:S(2)}) async-start(f32[64,24,256]{2,1,0:T(8,128)} %bitcast.70), calls=%async_computation | async-start | bytes 3145728 | tf_op jit(solution)/shard_map/all_to_all | solution.py:376
  112.1 41.1 %collective-permute-start.3 = (f32[512,128]{1,0:T(8,128)}, f32[512,128]{1,0:T(8,128)S(1)}, u32[]{:S(2)}, u32[]{:S(2)}) collective-permute-start(f32[512,128]{1,0:T(8,128)} %copy-done.4), channel_id=1, source_target_pairs={{0,1},{1,2},{2,3},{3,0},{4,5},{5,6},{6,7},{7,4},{8,9},{9,10},{10,1... | collective-permute-start | bytes 786440 | tf_op jit(solution)/shard_map/ppermute | solution.py:18
  112.2 41.1 %collective-permute-start.7 = (f32[512,128]{1,0:T(8,128)}, f32[512,128]{1,0:T(8,128)}, u32[]{:S(2)}, u32[]{:S(2)}) collective-permute-start(f32[512,128]{1,0:T(8,128)} %get-tuple-element.62), channel_id=1, source_target_pairs={{0,1},{1,2},{2,3},{3,0},{4,5},{5,6},{6,7},{7,4},{8,9},{9,10},{10,1... | collective-permute-start | bytes 786440 | tf_op jit(solution)/shard_map/ppermute | solution.py:18
  115.9 37.9 %collective-permute-start.24 = (f32[128,256]{1,0:T(8,128)}, f32[128,256]{1,0:T(8,128)}, u32[]{:S(2)}, u32[]{:S(2)}) collective-permute-start(f32[128,256]{1,0:T(8,128)} %get-tuple-element.87), channel_id=1, source_target_pairs={{0,3},{1,0},{2,1},{3,2},{4,7},{5,4},{6,5},{7,6},{8,11},{9,8},{10,9... | collective-permute-start | bytes 393224 | tf_op jit(solution)/shard_map/ppermute | solution.py:18
  118.7 37.9 %collective-permute-start.23 = (f32[128,256]{1,0:T(8,128)}, f32[128,256]{1,0:T(8,128)}, u32[]{:S(2)}, u32[]{:S(2)}) collective-permute-start(f32[128,256]{1,0:T(8,128)} %get-tuple-element.86), channel_id=1, source_target_pairs={{0,2},{1,3},{2,0},{3,1},{4,6},{5,7},{6,4},{7,5},{8,10},{9,11},{10,... | collective-permute-start | bytes 393224 | tf_op jit(solution)/shard_map/ppermute | solution.py:18
  120.1 38.0 %collective-permute-start.22 = (f32[128,256]{1,0:T(8,128)}, f32[128,256]{1,0:T(8,128)}, u32[]{:S(2)}, u32[]{:S(2)}) collective-permute-start(f32[128,256]{1,0:T(8,128)} %get-tuple-element.85), channel_id=1, source_target_pairs={{0,1},{1,2},{2,3},{3,0},{4,5},{5,6},{6,7},{7,4},{8,9},{9,10},{10,1... | collective-permute-start | bytes 393224 | tf_op jit(solution)/shard_map/ppermute | solution.py:18
  153.2 23.2 %collective-permute-start.11 = (f32[512,128]{1,0:T(8,128)S(1)}, f32[512,128]{1,0:T(8,128)S(1)}, u32[]{:S(2)}, u32[]{:S(2)}) collective-permute-start(f32[512,128]{1,0:T(8,128)S(1)} %copy-done.6), channel_id=1, source_target_pairs={{0,1},{1,2},{2,3},{3,0},{4,5},{5,6},{6,7},{7,4},{8,9},{9,10},{10,1... | collective-permute-start | bytes 786440 | tf_op jit(solution)/shard_map/ppermute | solution.py:18
  153.3 25.2 %collective-permute-start.15 = (f32[512,128]{1,0:T(8,128)S(1)}, f32[512,128]{1,0:T(8,128)S(1)}, u32[]{:S(2)}, u32[]{:S(2)}) collective-permute-start(f32[512,128]{1,0:T(8,128)S(1)} %copy-done.8), channel_id=1, source_target_pairs={{0,1},{1,2},{2,3},{3,0},{4,5},{5,6},{6,7},{7,4},{8,9},{9,10},{10,1... | collective-permute-start | bytes 786440 | tf_op jit(solution)/shard_map/ppermute | solution.py:18
  156.6 14.1 %collective-permute-start.17 = (f32[128,256]{1,0:T(8,128)S(1)}, f32[128,256]{1,0:T(8,128)S(1)}, u32[]{:S(2)}, u32[]{:S(2)}) collective-permute-start(f32[128,256]{1,0:T(8,128)S(1)} %get-tuple-element.81), channel_id=1, source_target_pairs={{0,2},{1,3},{2,0},{3,1},{4,6},{5,7},{6,4},{7,5},{8,10},{9,11},{10,... | collective-permute-start | bytes 393224 | tf_op jit(solution)/shard_map/ppermute | solution.py:18
  158.1 18.2 %collective-permute-start.16 = (f32[128,256]{1,0:T(8,128)S(1)}, f32[128,256]{1,0:T(8,128)S(1)}, u32[]{:S(2)}, u32[]{:S(2)}) collective-permute-start(f32[128,256]{1,0:T(8,128)S(1)} %get-tuple-element.80), channel_id=1, source_target_pairs={{0,1},{1,2},{2,3},{3,0},{4,5},{5,6},{6,7},{7,4},{8,9},{9,10},{10,1... | collective-permute-start | bytes 393224 | tf_op jit(solution)/shard_map/ppermute | solution.py:18
  160.5 20.2 %collective-permute-start.25 = (f32[128,256]{1,0:T(8,128)S(1)}, f32[128,256]{1,0:T(8,128)S(1)}, u32[]{:S(2)}, u32[]{:S(2)}) collective-permute-start(f32[128,256]{1,0:T(8,128)S(1)} %add_add_fusion.refs_0_), channel_id=1, source_target_pairs={{0,1},{1,2},{2,3},{3,0},{4,5},{5,6},{6,7},{7,4},{8,9},{9,10},{10,1... | collective-permute-start | bytes 393224 | tf_op jit(solution)/shard_map/ppermute | solution.py:18
  170.7 12.5 %collective-permute-start.26 = (f32[128,256]{1,0:T(8,128)S(1)}, f32[128,256]{1,0:T(8,128)S(1)}, u32[]{:S(2)}, u32[]{:S(2)}) collective-permute-start(f32[128,256]{1,0:T(8,128)S(1)} %add_add_fusion.refs_0_), channel_id=1, source_target_pairs={{0,2},{1,3},{2,0},{3,1},{4,6},{5,7},{6,4},{7,5},{8,10},{9,11},{10,... | collective-permute-start | bytes 393224 | tf_op jit(solution)/shard_map/ppermute | solution.py:18
  176.3 11.6 %collective-permute-start.19 = (f32[128,256]{1,0:T(8,128)S(1)}, f32[128,256]{1,0:T(8,128)S(1)}, u32[]{:S(2)}, u32[]{:S(2)}) collective-permute-start(f32[128,256]{1,0:T(8,128)S(1)} %add_add_fusion.1.refs_0_), channel_id=1, source_target_pairs={{0,1},{1,2},{2,3},{3,0},{4,5},{5,6},{6,7},{7,4},{8,9},{9,10},{10,1... | collective-permute-start | bytes 393224 | tf_op jit(solution)/shard_map/ppermute | solution.py:18
  178.4 9.5 %collective-permute-start.20 = (f32[128,256]{1,0:T(8,128)S(1)}, f32[128,256]{1,0:T(8,128)S(1)}, u32[]{:S(2)}, u32[]{:S(2)}) collective-permute-start(f32[128,256]{1,0:T(8,128)S(1)} %add_add_fusion.1.refs_0_), channel_id=1, source_target_pairs={{0,2},{1,3},{2,0},{3,1},{4,6},{5,7},{6,4},{7,5},{8,10},{9,11},{10,... | collective-permute-start | bytes 393224 | tf_op jit(solution)/shard_map/ppermute | solution.py:18
  (15 other events, 101.5 us)
